TPU v7x, 32 devices: a whole 2x2x4 slice. The times are simulated.
32 devices in a mesh: parts: 2 (over y), row: 4 (over z), col: 4 (over x, core), sub: 1.
Axes of the slice: x: 2, y: 2, z: 4, core: 2. Of those that a mesh axis runs over, the one named last changes fastest.
Arguments:
- activations: bfloat16 [1024, 2048], P(('parts', 'row'), ('col', 'sub')), parts along dimension 0, may hold values from -6 to 6
- expert_ids: int32 [1024, 8], P(('parts', 'row')), parts along dimension 0, may hold values from 0 to 15, all different within a row; in each aligned block of 32 rows (0 to 31, 32 to 63, ...) at most 32 rows name the same one
- gate_scores: float32 [1024, 8], P(('parts', 'row')), parts along dimension 0, may hold values from 0.05 to 0.5
- gate_proj: bfloat16 [16, 2048, 768], P(('row', 'col'), None, 'sub'), may hold values from -0.125 to 0.125
- up_proj: bfloat16 [16, 2048, 768], P(('row', 'col'), None, 'sub'), may hold values from -0.125 to 0.125
- down_proj: bfloat16 [16, 768, 2048], P(('row', 'col'), 'sub'), may hold values from -0.21875 to 0.21875
Outputs:
- moe_output: bfloat16 [1024, 2048], P(('parts', 'row'), ('col', 'sub')), parts along dimension 0
There are 2 independent parts, one for each index of `parts`. A program takes and returns all parts, laid end to end along the dimension named above; an argument that names none is the same for every part. Nothing has to cross between parts.
Inputs may be any that keep to these rules, and one draw needn't show every extreme that they name: `expert_ids`: each row names 8 different experts. In each aligned block of 32 rows no expert is named by more than 32 rows, a bound that some block reaches.
All inputs are finite; a program needn't handle non-finite values.
Results may differ from a plain program's by a relative error of at most 0.0057.
Values may be sent and summed in bfloat16 or wider, within the bound.
No kernel may reach another device: no remote copies, remote signals or barrier semaphores. Data moves between devices by JAX's collectives and lax.ppermute only.
A program may use at most 64 MiB of HBM per device.

v0:
```python
import jax
import jax.numpy as jnp
from jax import lax
from jax.sharding import PartitionSpec as P

TOP = 8


def slot_places(chosen, experts, capacity):
    count = chosen.shape[0] * chosen.shape[1]
    flat_ids = chosen.reshape(count)
    onehot = (flat_ids[:, None] == jnp.arange(experts, dtype=jnp.int32)[None, :]).astype(jnp.int32)
    running = jnp.cumsum(onehot, axis=0) - 1
    ranking = jnp.sum(onehot * running, axis=1)
    return flat_ids * capacity + ranking


def fill_slots(row_block, places, experts, capacity, top_count):
    owners = jnp.full((experts * capacity,), row_block.shape[0], jnp.int32)
    owners = owners.at[places].set(jnp.arange(places.shape[0], dtype=jnp.int32) // top_count)
    padded = jnp.concatenate(
        [row_block, jnp.zeros((1, row_block.shape[1]), row_block.dtype)], axis=0
    )
    return padded[owners].reshape(experts, capacity, row_block.shape[1])


def run_expert(stacked, gate_proj, up_proj, down_proj):
    layout = stacked.shape
    inputs = stacked.reshape(-1, layout[-1])
    gate_val = jnp.dot(inputs, gate_proj[0], preferred_element_type=jnp.float32)
    up_val = jnp.dot(inputs, up_proj[0], preferred_element_type=jnp.float32)
    hidden = (jax.nn.silu(gate_val) * up_val).astype(jnp.bfloat16)
    partial_out = jnp.dot(hidden, down_proj[0], preferred_element_type=jnp.float32)
    return partial_out.reshape(layout)


def send_back(stacked, gate_proj, up_proj, down_proj):
    partial_out = run_expert(stacked, gate_proj, up_proj, down_proj)
    landed = lax.all_to_all(partial_out, ("row", "col"), split_axis=1, concat_axis=1, tiled=True)
    return lax.psum_scatter(landed, "sub", scatter_dimension=0, tiled=True).astype(jnp.bfloat16)


def per_device(activations, expert_ids, gate_scores, gate_proj, up_proj, down_proj):
    col_count = lax.axis_size("col")
    sub_count = lax.axis_size("sub")
    experts = lax.axis_size("row") * col_count
    group_rows = expert_ids.shape[0]
    block_rows = group_rows // (col_count * sub_count)
    capacity = max(2, min(block_rows, 2 * block_rows * TOP // experts))
    quarter = sub_count * block_rows
    width = activations.shape[1] * col_count * sub_count
    whole = lax.all_gather(activations, ("col", "sub"), axis=1, tiled=True)
    col_start = lax.axis_index("col") * quarter
    sub_index = lax.axis_index("sub")
    my_rows = lax.dynamic_slice_in_dim(whole, col_start, quarter, 0)
    my_ids = lax.dynamic_slice_in_dim(expert_ids, col_start, quarter, 0)
    own_scores = lax.dynamic_slice_in_dim(
        gate_scores, col_start + sub_index * block_rows, block_rows, 0
    )
    places = []
    for member in range(sub_count):
        lower = member * block_rows
        places.append(slot_places(my_ids[lower : lower + block_rows], experts, capacity))
    own_places = lax.dynamic_index_in_dim(jnp.stack(places), sub_index, 0, keepdims=False)
    buffers = []
    for member in range(sub_count):
        lower = member * block_rows
        buffers.append(
            fill_slots(my_rows[lower : lower + block_rows], places[member], experts, capacity, TOP)
        )
    outgoing = jnp.stack(buffers)
    returned = send_back(
        lax.all_to_all(outgoing, ("row", "col"), split_axis=1, concat_axis=1, tiled=True),
        gate_proj,
        up_proj,
        down_proj,
    )
    picked = returned.reshape(-1, width)[own_places].reshape(block_rows, TOP, width)
    share = jnp.sum(own_scores[:, :, None] * picked.astype(jnp.float32), axis=1)
    return lax.all_to_all(
        share.astype(jnp.bfloat16), ("col", "sub"), split_axis=1, concat_axis=0, tiled=True
    )


def solution(mesh):
    placed = (
        P(("parts", "row"), ("col", "sub")),
        P(("parts", "row"), None),
        P(("parts", "row"), None),
        P(("row", "col"), None, "sub"),
        P(("row", "col"), None, "sub"),
        P(("row", "col"), "sub", None),
    )
    return jax.shard_map(
        per_device,
        mesh=mesh,
        in_specs=placed,
        out_specs=P(("parts", "row"), ("col", "sub")),
        check_vma=False,
    )
```

profile of v0, /device:TPU:20, one launch (start us, length us, event | category | flops | bytes accessed | tf_op | source)
XLA Modules:
  0.0 142.7 jit_solution(10261888234593727119)
XLA Ops:
  0.0 0.9 broadcast_multiply_fusion
  0.9 0.1 copy.21
  1.0 0.1 eq.29
  1.1 0.1 eq.25
  1.2 0.6 reduce-window.6
  1.8 0.2 slice_reduce_fusion
  2.0 0.1 copy.20
  2.1 0.1 mul.43
  2.2 0.1 fusion.9
  2.3 1.4 scatter_custom_fusion
  3.7 7.4 %all_gather.3 = bf16[128,2048]{1,0:T(8,128)(2,1)S(1)} all-gather(bf16[128,512]{1,0:T(8,128)(2,1)} %param.6), channel_id=1, replica_groups=mesh['parts'=2,'row'=4,'col'=4,'sub'=1] {'col','sub'}, dimensions={1}, use_global_device_ids=true | all-gather | bytes 655360 | tf_op jit(solution)/shard_map/all_gather | solution.py:52
  11.1 3.3 %gather_fusion = bf16[512,2048]{1,0:T(8,128)(2,1)} fusion(bf16[33,2048]{1,0:T(8,128)(2,1)S(1)} %concatenate.3, s32[1024]{0:T(1024)S(1)} %pad_clamp_fusion.1), kind=kCustom, calls=%fused_computation | custom fusion | bytes 4196352 | tf_op jit(solution)/shard_map/gather | solution.py:24
  14.5 53.6 %all_to_all.26 = bf16[1,16,32,2048]{3,2,0,1:T(8,128)(2,1)S(1)} all-to-all(bf16[1,16,32,2048]{3,2,0,1:T(8,128)(2,1)} %bitcast.52), channel_id=1, replica_groups=mesh['parts'=2,'row'=4,'col'=4,'sub'=1] {'row','col'}, dimensions={1} | all-to-all | bytes 4194304 | tf_op jit(solution)/shard_map/all_to_all | solution.py:73
  68.1 1.8 %fusion.3 = f32[512,768]{1,0:T(8,128)S(1)} fusion(bf16[512,2048]{1,0:T(8,128)(2,1)S(1)} %bitcast.53, bf16[1,2048,768]{2,1,0:T(8,128)(2,1)S(1)} %copy-done.2), kind=kOutput, calls=%fused_computation.7 | convolution fusion | flops 1610612736 | bytes 6815744 | tf_op jit(solution)/shard_map/dot_general | solution.py:30
  69.9 1.9 %multiply_convert_fusion = bf16[512,768]{1,0:T(8,128)(2,1)S(1)} fusion(f32[512,768]{1,0:T(8,128)S(1)} %fusion.3, bf16[512,2048]{1,0:T(8,128)(2,1)S(1)} %bitcast.54, bf16[1,2048,768]{2,1,0:T(8,128)(2,1)S(1)} %copy-done.3), kind=kOutput, calls=%fused_computation.11 | convolution fusion | flops 1612972032 | bytes 7602176 | tf_op jit(solution)/shard_map/dot_general | solution.py:31
  71.9 3.1 %convolution_bitcast_fusion = bf16[1,16,32,2048]{3,2,0,1:T(8,128)(2,1)} fusion(bf16[16,32,768]{2,1,0:T(8,128)(2,1)S(1)} %bitcast.61, bf16[1,768,2048]{2,1,0:T(8,128)(2,1)S(1)} %copy-done), kind=kOutput, calls=%fused_computation.3 | convolution fusion | flops 1610612736 | bytes 6029312 | tf_op jit(solution)/shard_map/dot_general | solution.py:33
  75.0 4.9 %all-to-all-start.1 = ((bf16[1,16,32,2048]{3,2,0,1:T(8,128)(2,1)}), bf16[1,16,32,2048]{3,2,0,1:T(8,128)(2,1)}, u32[]{:S(2)}, u32[]{:S(2)}) async-start(bf16[1,16,32,2048]{3,2,0,1:T(8,128)(2,1)} %convolution_bitcast_fusion), calls=%async_computation.1 | async-start | bytes 4194304 | tf_op jit(solution)/shard_map/all_to_all | solution.py:39
  79.9 0.1 constant_dynamic-slice_fusion.2
  80.0 0.1 copy.19
  80.0 47.6 %all-to-all-done.1 = bf16[1,16,32,2048]{3,2,0,1:T(8,128)(2,1)} async-done(((bf16[1,16,32,2048]{3,2,0,1:T(8,128)(2,1)}), bf16[1,16,32,2048]{3,2,0,1:T(8,128)(2,1)}, u32[]{:S(2)}, u32[]{:S(2)}) %all-to-all-start.1) | async-done | bytes 2097184 | tf_op jit(solution)/shard_map/all_to_all | solution.py:39
  127.6 5.2 %gather_fusion.1 = bf16[256,2048]{1,0:T(8,128)(2,1)} fusion(bf16[512,2048]{1,0:T(8,128)(2,1)} %bitcast.13, s32[1024]{0:T(1024)S(1)} %pad_clamp_fusion), kind=kCustom, calls=%fused_computation.1 | custom fusion | bytes 2098176 | tf_op jit(solution)/shard_map/gather | solution.py:78
  132.8 2.2 %fusion.5 = bf16[32,2048]{1,0:T(8,128)(2,1)S(1)} fusion(bf16[256,2048]{1,0:T(8,128)(2,1)} %gather_fusion.1, f32[32,8]{1,0:T(8,128)S(1)} %copy.19), kind=kLoop, calls=%fused_computation.10 | loop fusion | flops 1507328 | bytes 1180672 | tf_op jit(solution)/shard_map/reduce_sum | solution.py:79
  135.0 7.0 %all_to_all.27 = bf16[32,4,512]{2,0,1:T(8,128)(2,1)S(1)} all-to-all(bf16[32,4,512]{2,0,1:T(8,128)(2,1)S(1)} %bitcast.56), channel_id=1, replica_groups=mesh['parts'=2,'row'=4,'col'=4,'sub'=1] {'col','sub'}, dimensions={1} | all-to-all | bytes 262144 | tf_op jit(solution)/shard_map/all_to_all | solution.py:80
  142.0 0.7 copy.33
  (19 shorter events, 0.2 us)
Async XLA Ops:
  0.0 71.9 %copy-start = (bf16[1,768,2048]{2,1,0:T(8,128)(2,1)S(1)}, bf16[1,768,2048]{2,1,0:T(8,128)(2,1)}, u32[]{:S(2)}) copy-start(bf16[1,768,2048]{2,1,0:T(8,128)(2,1)} %param.11) | copy-start | bytes 9437188
  14.5 53.6 %copy-start.2 = (bf16[1,2048,768]{2,1,0:T(8,128)(2,1)S(1)}, bf16[1,2048,768]{2,1,0:T(8,128)(2,1)}, u32[]{:S(2)}) copy-start(bf16[1,2048,768]{2,1,0:T(8,128)(2,1)} %param.9) | copy-start | bytes 9437188
  68.1 1.9 %copy-start.3 = (bf16[1,2048,768]{2,1,0:T(8,128)(2,1)S(1)}, bf16[1,2048,768]{2,1,0:T(8,128)(2,1)}, u32[]{:S(2)}) copy-start(bf16[1,2048,768]{2,1,0:T(8,128)(2,1)} %param.10) | copy-start | bytes 9437188
  75.0 4.9 %copy-start.1 = (f32[128,8]{0,1:T(8,128)S(1)}, f32[128,8]{0,1:T(8,128)}, u32[]{:S(2)}) copy-start(f32[128,8]{0,1:T(8,128)} %param.8) | copy-start | bytes 12292
  75.0 52.6 %all-to-all-start.1 = ((bf16[1,16,32,2048]{3,2,0,1:T(8,128)(2,1)}), bf16[1,16,32,2048]{3,2,0,1:T(8,128)(2,1)}, u32[]{:S(2)}, u32[]{:S(2)}) async-start(bf16[1,16,32,2048]{3,2,0,1:T(8,128)(2,1)} %convolution_bitcast_fusion), calls=%async_computation.1 | async-start | bytes 4194304 | tf_op jit(solution)/shard_map/all_to_all | solution.py:39
where the time goes:
time: 143 us
  blocking collectives  67.9 us (47%)
  waiting for transfers between devices  47.6 us (33%)
  local copies, waits for them, and re-layouts  11.5 us (8%)
  matrix products  6.85 us (5%)
  starting transfers between devices  4.86 us (3%)
  other arithmetic  3.86 us (3%)
    all_to_all x1, blocking collectives, per_device(): lax.all_to_all(outgoing, ('row', 'col'), split_axis=1, concat_axis=1, til...  53.6 us
    all_to_all x1, waiting for transfers between devices, send_back(): lax.all_to_all(partial_out, ('row', 'col'), split_axis=1, concat_axis=1,...  47.6 us
    all_gather x1, blocking collectives, per_device(): whole = lax.all_gather(activations, ('col', 'sub'), axis=1, tiled=True)  7.38 us
    all_to_all x1, blocking collectives, per_device(): lax.all_to_all(share.astype(jnp.bfloat16), ('col', 'sub'), split_axis=1,...  6.99 us
    gather x1, local copies, waits for them, and re-layouts, per_device(): returned.reshape(-1, width)[own_places].reshape(block_rows, TOP, width)  5.21 us
    all_to_all x1, starting transfers between devices, send_back(): lax.all_to_all(partial_out, ('row', 'col'), split_axis=1, concat_axis=1,...  4.86 us
    gather x1, local copies, waits for them, and re-layouts, fill_slots(): return padded[owners].reshape(experts, capacity, row_block.shape[1])  3.35 us
    dot_general x1, matrix products, run_expert(): jnp.dot(hidden, down_proj[0], preferred_element_type=jnp.float32)  3.14 us
  transfers between devices with their start and end apart: 1, of which 1 were waited for; matrix products, arithmetic and copies ran while one was open for 0% of the time, Pallas kernels for 0%

commit v1 on v0

--- a/solution.py
+++ b/solution.py
@@ -4,6 +4,29 @@
 from jax.sharding import PartitionSpec as P
 
 TOP = 8
+
+
+def split_up(x, dim, size):
+    lengths = x.shape
+    parts = x.reshape(*lengths[:dim], size, lengths[dim] // size, *lengths[dim + 1 :])
+    return jnp.moveaxis(parts, dim, 0)
+
+
+def joined_along(blocks, dim):
+    blocks = jnp.moveaxis(blocks, 0, dim)
+    dims = blocks.shape
+    return blocks.reshape(*dims[:dim], dims[dim] * dims[dim + 1], *dims[dim + 2 :])
+
+
+def swapped_with_each(x, axis, split_dim, concat_dim):
+    size, index = (lax.axis_size(axis), lax.axis_index(axis))
+    parts = split_up(x, split_dim, size)
+    done = [parts[index]]
+    for turn in range(1, size):
+        sent = parts[index ^ turn]
+        done.append(lax.ppermute(sent, axis, [(i, i ^ turn) for i in range(size)]))
+    parts = jnp.stack(done)[index ^ jnp.arange(size)]
+    return joined_along(parts, concat_dim)
 
 
 def slot_places(chosen, experts, capacity):
@@ -70,10 +93,7 @@
         )
     outgoing = jnp.stack(buffers)
     returned = send_back(
-        lax.all_to_all(outgoing, ("row", "col"), split_axis=1, concat_axis=1, tiled=True),
-        gate_proj,
-        up_proj,
-        down_proj,
+        swapped_with_each(outgoing, ("row", "col"), 1, 1), gate_proj, up_proj, down_proj
     )
     picked = returned.reshape(-1, width)[own_places].reshape(block_rows, TOP, width)
     share = jnp.sum(own_scores[:, :, None] * picked.astype(jnp.float32), axis=1)

time: 143 us -> 157 us (1.098)
  blocking collectives: 67.9 us -> 14.4 us
  waiting for transfers between devices: 47.6 us -> 75.2 us
  starting transfers between devices: 4.86 us -> 25.7 us
  local copies, waits for them, and re-layouts: 11.5 us -> 27.3 us
  matrix products: 6.85 us -> 9.5 us
    all_to_all x1 -> x0, blocking collectives: 53.6 us -> none  [per_device(): lax.all_to_all(outgoing, ('row', 'col'), split_axis=1, concat_axis=1, til...]
    ppermute x0 -> x15, waiting for transfers between devices: none -> 27.7 us  [swapped_with_each(): done.append(lax.ppermute(sent, axis, [(i, i ^ turn) for i in range(size)]))]
    ppermute x0 -> x15, starting transfers between devices: none -> 21 us  [swapped_with_each(): done.append(lax.ppermute(sent, axis, [(i, i ^ turn) for i in range(size)]))]
    unnamed x9 -> x23, local copies, waits for them, and re-layouts: 0.74 us -> 9.92 us
    gather x0 -> x1, local copies, waits for them, and re-layouts: none -> 3.58 us  [swapped_with_each(): parts = jnp.stack(done)[index ^ jnp.arange(size)]]
    dot_general x1, matrix products: 1.81 us -> 4.45 us  [run_expert(): gate_val = jnp.dot(inputs, gate_proj[0], preferred_element_type=jnp.float32)]
    squeeze x0 -> x1, local copies, waits for them, and re-layouts: none -> 2.42 us  [swapped_with_each(): sent = parts[index ^ turn]]
  transfers between devices with their start and end apart: 1 -> 16, of which waited for: 1 -> 9; matrix products, arithmetic and copies ran while one was open for 0% -> 6% of each run, Pallas kernels for 0% -> 0%
where the time goes in v1:
time: 157 us; the launch traced here: 156 us
  waiting for transfers between devices  75.2 us (48%)
  local copies, waits for them, and re-layouts  27.3 us (17%)
  starting transfers between devices  25.7 us (16%)
  blocking collectives  14.4 us (9%)
  matrix products  9.5 us (6%)
  other arithmetic  3.87 us (2%)
    all_to_all x1, waiting for transfers between devices, send_back(): lax.all_to_all(partial_out, ('row', 'col'), split_axis=1, concat_axis=1,...  47.6 us
    ppermute x15, waiting for transfers between devices, swapped_with_each(): done.append(lax.ppermute(sent, axis, [(i, i ^ turn) for i in range(size)]))  27.7 us
    ppermute x15, starting transfers between devices, swapped_with_each(): done.append(lax.ppermute(sent, axis, [(i, i ^ turn) for i in range(size)]))  21 us
    unnamed x23, local copies, waits for them, and re-layouts  9.92 us
    all_gather x1, blocking collectives, per_device(): whole = lax.all_gather(activations, ('col', 'sub'), axis=1, tiled=True)  7.38 us
    all_to_all x1, blocking collectives, per_device(): lax.all_to_all(share.astype(jnp.bfloat16), ('col', 'sub'), split_axis=1,...  6.99 us
    gather x1, local copies, waits for them, and re-layouts, per_device(): returned.reshape(-1, width)[own_places].reshape(block_rows, TOP, width)  5.23 us
    all_to_all x1, starting transfers between devices, send_back(): lax.all_to_all(partial_out, ('row', 'col'), split_axis=1, concat_axis=1,...  4.72 us
  transfers between devices with their start and end apart: 16, of which 9 were waited for; matrix products, arithmetic and copies ran while one was open for 6% of the time, Pallas kernels for 0%

profile of v1, /device:TPU:20, one launch (start us, length us, event | category | flops | bytes accessed | tf_op | source)
XLA Modules:
  0.0 156.2 jit_solution(4643887677983675680)
XLA Ops:
  3.8 7.4 %all_gather.3 = bf16[128,2048]{1,0:T(8,128)(2,1)S(1)} all-gather(bf16[128,512]{1,0:T(8,128)(2,1)} %param.6), channel_id=1, replica_groups=mesh['parts'=2,'row'=4,'col'=4,'sub'=1] {'col','sub'}, dimensions={1}, use_global_device_ids=true | all-gather | bytes 655360 | tf_op jit(solution)/shard_map/all_gather | solution.py:75
  11.2 3.3 %gather_fusion = bf16[512,2048]{1,0:T(8,128)(2,1)} fusion(bf16[33,2048]{1,0:T(8,128)(2,1)S(1)} %concatenate.3, s32[1024]{0:T(1024)S(1)} %pad_clamp_fusion.2), kind=kCustom, calls=%fused_computation | custom fusion | bytes 4196352 | tf_op jit(solution)/shard_map/gather | solution.py:47
  14.5 2.4 %dynamic-slice_bitcast_fusion = (bf16[1,1,32,2048]{3,2,1,0:T(8,128)(2,1)S(1)}, bf16[1,1,32,2048]{3,2,1,0:T(8,128)(2,1)S(1)}, bf16[1,1,32,2048]{3,2,1,0:T(8,128)(...) fusion(bf16[16,1,1,32,2048]{4,3,0,2,1:T(8,128)(2,1)} %bitcast.1, ...), kind=kLoop, calls=%fused_computation.29 | loop fusion | bytes 4194368 | tf_op jit(solution)/shard_map/squeeze | solution.py:26
  20.8 2.2 %collective-permute-start.5 = (bf16[1,1,32,2048]{3,2,1,0:T(8,128)(2,1)S(1)}, bf16[1,1,32,2048]{3,2,1,0:T(8,128)(2,1)S(1)}, u32[]{:S(2)}, u32[]{:S(2)}) collective-permute-start(bf16[1,1,32,2048]{3,2,1,0:T(8,128)(2,1)S(1)} %get-tuple-element.16), channel_id=1, source_target_pairs={{0,6},{1,7},{2,4},{3,5},{4,2},{5,3},{6,0},{7,1},{8,14},{9,15},{10,... | collective-permute-start | bytes 393224 | tf_op jit(solution)/shard_map/ppermute | solution.py:27
  25.8 3.6 %collective-permute-start.8 = (bf16[1,1,32,2048]{3,2,1,0:T(8,128)(2,1)S(1)}, bf16[1,1,32,2048]{3,2,1,0:T(8,128)(2,1)S(1)}, u32[]{:S(2)}, u32[]{:S(2)}) collective-permute-start(bf16[1,1,32,2048]{3,2,1,0:T(8,128)(2,1)S(1)} %get-tuple-element.13), channel_id=1, source_target_pairs={{0,9},{1,8},{2,11},{3,10},{4,13},{5,12},{6,15},{7,14},{8,1},{9,0},... | collective-permute-start | bytes 393224 | tf_op jit(solution)/shard_map/ppermute | solution.py:27
  31.5 2.2 %collective-permute-done.5 = bf16[1,1,32,2048]{3,2,1,0:T(8,128)(2,1)S(1)} collective-permute-done((bf16[1,1,32,2048]{3,2,1,0:T(8,128)(2,1)S(1)}, bf16[1,1,32,2048]{3,2,1,0:T(8,128)(2,1)S(1)}, u32[]{:S(2)}, u32[]{:S(2)}) %collective-permute-start.5) | collective-permute-done | bytes 131104 | tf_op jit(solution)/shard_map/ppermute | solution.py:27
  33.7 3.4 %collective-permute-start.10 = (bf16[1,1,32,2048]{3,2,1,0:T(8,128)(2,1)S(1)}, bf16[1,1,32,2048]{3,2,1,0:T(8,128)(2,1)S(1)}, u32[]{:S(2)}, u32[]{:S(2)}) collective-permute-start(bf16[1,1,32,2048]{3,2,1,0:T(8,128)(2,1)S(1)} %get-tuple-element.11), channel_id=1, source_target_pairs={{0,11},{1,10},{2,9},{3,8},{4,15},{5,14},{6,13},{7,12},{8,3},{9,2},... | collective-permute-start | bytes 393224 | tf_op jit(solution)/shard_map/ppermute | solution.py:27
  38.9 1.9 %collective-permute-start.12 = (bf16[1,1,32,2048]{3,2,1,0:T(8,128)(2,1)S(1)}, bf16[1,1,32,2048]{3,2,1,0:T(8,128)(2,1)S(1)}, u32[]{:S(2)}, u32[]{:S(2)}) collective-permute-start(bf16[1,1,32,2048]{3,2,1,0:T(8,128)(2,1)S(1)} %get-tuple-element.9), channel_id=1, source_target_pairs={{0,13},{1,12},{2,15},{3,14},{4,9},{5,8},{6,11},{7,10},{8,5},{9,4},... | collective-permute-start | bytes 393224 | tf_op jit(solution)/shard_map/ppermute | solution.py:27
  41.5 8.1 %collective-permute-done.8 = bf16[1,1,32,2048]{3,2,1,0:T(8,128)(2,1)S(1)} collective-permute-done((bf16[1,1,32,2048]{3,2,1,0:T(8,128)(2,1)S(1)}, bf16[1,1,32,2048]{3,2,1,0:T(8,128)(2,1)S(1)}, u32[]{:S(2)}, u32[]{:S(2)}) %collective-permute-start.8) | collective-permute-done | bytes 131104 | tf_op jit(solution)/shard_map/ppermute | solution.py:27
  49.6 2.4 %collective-permute-start.13 = (bf16[1,1,32,2048]{3,2,1,0:T(8,128)(2,1)S(1)}, bf16[1,1,32,2048]{3,2,1,0:T(8,128)(2,1)S(1)}, u32[]{:S(2)}, u32[]{:S(2)}) collective-permute-start(bf16[1,1,32,2048]{3,2,1,0:T(8,128)(2,1)S(1)} %get-tuple-element.8), channel_id=1, source_target_pairs={{0,14},{1,15},{2,12},{3,13},{4,10},{5,11},{6,8},{7,9},{8,6},{9,7},... | collective-permute-start | bytes 393224 | tf_op jit(solution)/shard_map/ppermute | solution.py:27
  55.1 3.0 %collective-permute-done.10 = bf16[1,1,32,2048]{3,2,1,0:T(8,128)(2,1)S(1)} collective-permute-done((bf16[1,1,32,2048]{3,2,1,0:T(8,128)(2,1)S(1)}, bf16[1,1,32,2048]{3,2,1,0:T(8,128)(2,1)S(1)}, u32[]{:S(2)}, u32[]{:S(2)}) %collective-permute-start.10) | collective-permute-done | bytes 131104 | tf_op jit(solution)/shard_map/ppermute | solution.py:27
  58.8 7.2 %collective-permute-done.11 = bf16[1,1,32,2048]{3,2,1,0:T(8,128)(2,1)S(1)} collective-permute-done((bf16[1,1,32,2048]{3,2,1,0:T(8,128)(2,1)S(1)}, bf16[1,1,32,2048]{3,2,1,0:T(8,128)(2,1)S(1)}, u32[]{:S(2)}, u32[]{:S(2)}) %collective-permute-start.11) | collective-permute-done | bytes 131104 | tf_op jit(solution)/shard_map/ppermute | solution.py:27
  66.6 2.1 %collective-permute-done.12 = bf16[1,1,32,2048]{3,2,1,0:T(8,128)(2,1)S(1)} collective-permute-done((bf16[1,1,32,2048]{3,2,1,0:T(8,128)(2,1)S(1)}, bf16[1,1,32,2048]{3,2,1,0:T(8,128)(2,1)S(1)}, u32[]{:S(2)}, u32[]{:S(2)}) %collective-permute-start.12) | collective-permute-done | bytes 131104 | tf_op jit(solution)/shard_map/ppermute | solution.py:27
  69.3 2.8 %collective-permute-done.13 = bf16[1,1,32,2048]{3,2,1,0:T(8,128)(2,1)S(1)} collective-permute-done((bf16[1,1,32,2048]{3,2,1,0:T(8,128)(2,1)S(1)}, bf16[1,1,32,2048]{3,2,1,0:T(8,128)(2,1)S(1)}, u32[]{:S(2)}, u32[]{:S(2)}) %collective-permute-start.13) | collective-permute-done | bytes 131104 | tf_op jit(solution)/shard_map/ppermute | solution.py:27
  72.8 2.0 %collective-permute-done.14 = bf16[1,1,32,2048]{3,2,1,0:T(8,128)(2,1)S(1)} collective-permute-done((bf16[1,1,32,2048]{3,2,1,0:T(8,128)(2,1)S(1)}, bf16[1,1,32,2048]{3,2,1,0:T(8,128)(2,1)S(1)}, u32[]{:S(2)}, u32[]{:S(2)}) %collective-permute-start.14) | collective-permute-done | bytes 131104 | tf_op jit(solution)/shard_map/ppermute | solution.py:27
  75.5 3.6 %gather_fusion.1 = bf16[16,32,2048]{2,1,0:T(8,128)(2,1)} fusion(bf16[16,32,2048]{2,1,0:T(8,128)(2,1)} %bitcast.34, s32[1024]{0:T(1024)S(1)} %pad_clamp_fusion.1), kind=kCustom, calls=%fused_computation.1 | custom fusion | bytes 4194368 | tf_op jit(solution)/shard_map/gather | solution.py:28
  79.1 4.5 %fusion.3 = f32[512,768]{1,0:T(8,128)S(1)} fusion(bf16[512,2048]{1,0:T(8,128)(2,1)} %bitcast.114, bf16[1,2048,768]{2,1,0:T(8,128)(2,1)} %param.9), kind=kOutput, calls=%fused_computation.8 | convolution fusion | flops 1610612736 | bytes 6815744 | tf_op jit(solution)/shard_map/dot_general | solution.py:53
  83.6 1.9 %multiply_convert_fusion = bf16[512,768]{1,0:T(8,128)(2,1)S(1)} fusion(f32[512,768]{1,0:T(8,128)S(1)} %fusion.3, bf16[512,2048]{1,0:T(8,128)(2,1)S(1)} %bitcast.115, bf16[1,2048,768]{2,1,0:T(8,128)(2,1)S(1)} %copy-done.3), kind=kOutput, calls=%fused_computation.12 | convolution fusion | flops 1612972032 | bytes 7602176 | tf_op jit(solution)/shard_map/dot_general | solution.py:54
  85.5 3.2 %convolution_bitcast_fusion = bf16[1,16,32,2048]{3,2,0,1:T(8,128)(2,1)} fusion(bf16[16,32,768]{2,1,0:T(8,128)(2,1)S(1)} %bitcast.122, bf16[1,768,2048]{2,1,0:T(8,128)(2,1)S(1)} %copy-done), kind=kOutput, calls=%fused_computation.4 | convolution fusion | flops 1610612736 | bytes 6029312 | tf_op jit(solution)/shard_map/dot_general | solution.py:56
  88.6 4.7 %all-to-all-start = ((bf16[1,16,32,2048]{3,2,0,1:T(8,128)(2,1)}), bf16[1,16,32,2048]{3,2,0,1:T(8,128)(2,1)}, u32[]{:S(2)}, u32[]{:S(2)}) async-start(bf16[1,16,32,2048]{3,2,0,1:T(8,128)(2,1)} %convolution_bitcast_fusion), calls=%async_computation | async-start | bytes 4194304 | tf_op jit(solution)/shard_map/all_to_all | solution.py:62
  93.5 47.6 %all-to-all-done = bf16[1,16,32,2048]{3,2,0,1:T(8,128)(2,1)} async-done(((bf16[1,16,32,2048]{3,2,0,1:T(8,128)(2,1)}), bf16[1,16,32,2048]{3,2,0,1:T(8,128)(2,1)}, u32[]{:S(2)}, u32[]{:S(2)}) %all-to-all-start) | async-done | bytes 2097184 | tf_op jit(solution)/shard_map/all_to_all | solution.py:62
  141.1 5.2 %gather_fusion.2 = bf16[256,2048]{1,0:T(8,128)(2,1)} fusion(bf16[512,2048]{1,0:T(8,128)(2,1)} %bitcast.44, s32[1024]{0:T(1024)S(1)} %pad_clamp_fusion), kind=kCustom, calls=%fused_computation.2 | custom fusion | bytes 2098176 | tf_op jit(solution)/shard_map/gather | solution.py:98
  146.3 2.2 %fusion.5 = bf16[32,2048]{1,0:T(8,128)(2,1)S(1)} fusion(bf16[256,2048]{1,0:T(8,128)(2,1)} %gather_fusion.2, f32[32,8]{1,0:T(8,128)S(1)} %copy.19), kind=kLoop, calls=%fused_computation.11 | loop fusion | flops 1507328 | bytes 1180672 | tf_op jit(solution)/shard_map/reduce_sum | solution.py:99
  148.5 7.0 %all_to_all.21 = bf16[32,4,512]{2,0,1:T(8,128)(2,1)S(1)} all-to-all(bf16[32,4,512]{2,0,1:T(8,128)(2,1)S(1)} %bitcast.117), channel_id=1, replica_groups=mesh['parts'=2,'row'=4,'col'=4,'sub'=1] {'col','sub'}, dimensions={1} | all-to-all | bytes 262144 | tf_op jit(solution)/shard_map/all_to_all | solution.py:100
  (67 shorter events, 22.2 us)
Async XLA Ops:
  0.0 85.5 %copy-start = (bf16[1,768,2048]{2,1,0:T(8,128)(2,1)S(1)}, bf16[1,768,2048]{2,1,0:T(8,128)(2,1)}, u32[]{:S(2)}) copy-start(bf16[1,768,2048]{2,1,0:T(8,128)(2,1)} %param.11) | copy-start | bytes 9437188
  16.9 3.9 %collective-permute-start = (bf16[1,1,32,2048]{3,2,1,0:T(8,128)(2,1)S(1)}, bf16[1,1,32,2048]{3,2,1,0:T(8,128)(2,1)S(1)}, u32[]{:S(2)}, u32[]{:S(2)}) collective-permute-start(bf16[1,1,32,2048]{3,2,1,0:T(8,128)(2,1)S(1)} %get-tuple-element.21), channel_id=1, source_target_pairs={{0,1},{1,0},{2,3},{3,2},{4,5},{5,4},{6,7},{7,6},{8,9},{9,8},{10,11... | collective-permute-start | bytes 393224 | tf_op jit(solution)/shard_map/ppermute | solution.py:27
  17.3 6.4 %collective-permute-start.1 = (bf16[1,1,32,2048]{3,2,1,0:T(8,128)(2,1)S(1)}, bf16[1,1,32,2048]{3,2,1,0:T(8,128)(2,1)S(1)}, u32[]{:S(2)}, u32[]{:S(2)}) collective-permute-start(bf16[1,1,32,2048]{3,2,1,0:T(8,128)(2,1)S(1)} %get-tuple-element.20), channel_id=1, source_target_pairs={{0,2},{1,3},{2,0},{3,1},{4,6},{5,7},{6,4},{7,5},{8,10},{9,11},{10,... | collective-permute-start | bytes 393224 | tf_op jit(solution)/shard_map/ppermute | solution.py:27
  18.4 6.5 %collective-permute-start.2 = (bf16[1,1,32,2048]{3,2,1,0:T(8,128)(2,1)S(1)}, bf16[1,1,32,2048]{3,2,1,0:T(8,128)(2,1)S(1)}, u32[]{:S(2)}, u32[]{:S(2)}) collective-permute-start(bf16[1,1,32,2048]{3,2,1,0:T(8,128)(2,1)S(1)} %get-tuple-element.19), channel_id=1, source_target_pairs={{0,3},{1,2},{2,1},{3,0},{4,7},{5,6},{6,5},{7,4},{8,11},{9,10},{10,... | collective-permute-start | bytes 393224 | tf_op jit(solution)/shard_map/ppermute | solution.py:27
  18.8 7.0 %collective-permute-start.3 = (bf16[1,1,32,2048]{3,2,1,0:T(8,128)(2,1)S(1)}, bf16[1,1,32,2048]{3,2,1,0:T(8,128)(2,1)S(1)}, u32[]{:S(2)}, u32[]{:S(2)}) collective-permute-start(bf16[1,1,32,2048]{3,2,1,0:T(8,128)(2,1)S(1)} %get-tuple-element.18), channel_id=1, source_target_pairs={{0,4},{1,5},{2,6},{3,7},{4,0},{5,1},{6,2},{7,3},{8,12},{9,13},{10,... | collective-permute-start | bytes 393224 | tf_op jit(solution)/shard_map/ppermute | solution.py:27
  20.4 9.7 %collective-permute-start.4 = (bf16[1,1,32,2048]{3,2,1,0:T(8,128)(2,1)S(1)}, bf16[1,1,32,2048]{3,2,1,0:T(8,128)(2,1)S(1)}, u32[]{:S(2)}, u32[]{:S(2)}) collective-permute-start(bf16[1,1,32,2048]{3,2,1,0:T(8,128)(2,1)S(1)} %get-tuple-element.17), channel_id=1, source_target_pairs={{0,5},{1,4},{2,7},{3,6},{4,1},{5,0},{6,3},{7,2},{8,13},{9,12},{10,... | collective-permute-start | bytes 393224 | tf_op jit(solution)/shard_map/ppermute | solution.py:27
  20.8 12.9 %collective-permute-start.5 = (bf16[1,1,32,2048]{3,2,1,0:T(8,128)(2,1)S(1)}, bf16[1,1,32,2048]{3,2,1,0:T(8,128)(2,1)S(1)}, u32[]{:S(2)}, u32[]{:S(2)}) collective-permute-start(bf16[1,1,32,2048]{3,2,1,0:T(8,128)(2,1)S(1)} %get-tuple-element.16), channel_id=1, source_target_pairs={{0,6},{1,7},{2,4},{3,5},{4,2},{5,3},{6,0},{7,1},{8,14},{9,15},{10,... | collective-permute-start | bytes 393224 | tf_op jit(solution)/shard_map/ppermute | solution.py:27
  23.6 14.1 %collective-permute-start.6 = (bf16[1,1,32,2048]{3,2,1,0:T(8,128)(2,1)S(1)}, bf16[1,1,32,2048]{3,2,1,0:T(8,128)(2,1)S(1)}, u32[]{:S(2)}, u32[]{:S(2)}) collective-permute-start(bf16[1,1,32,2048]{3,2,1,0:T(8,128)(2,1)S(1)} %get-tuple-element.15), channel_id=1, source_target_pairs={{0,7},{1,6},{2,5},{3,4},{4,3},{5,2},{6,1},{7,0},{8,15},{9,14},{10,... | collective-permute-start | bytes 393224 | tf_op jit(solution)/shard_map/ppermute | solution.py:27
  24.8 14.1 %collective-permute-start.7 = (bf16[1,1,32,2048]{3,2,1,0:T(8,128)(2,1)S(1)}, bf16[1,1,32,2048]{3,2,1,0:T(8,128)(2,1)S(1)}, u32[]{:S(2)}, u32[]{:S(2)}) collective-permute-start(bf16[1,1,32,2048]{3,2,1,0:T(8,128)(2,1)S(1)} %get-tuple-element.14), channel_id=1, source_target_pairs={{0,8},{1,9},{2,10},{3,11},{4,12},{5,13},{6,14},{7,15},{8,0},{9,1},... | collective-permute-start | bytes 393224 | tf_op jit(solution)/shard_map/ppermute | solution.py:27
  25.8 23.7 %collective-permute-start.8 = (bf16[1,1,32,2048]{3,2,1,0:T(8,128)(2,1)S(1)}, bf16[1,1,32,2048]{3,2,1,0:T(8,128)(2,1)S(1)}, u32[]{:S(2)}, u32[]{:S(2)}) collective-permute-start(bf16[1,1,32,2048]{3,2,1,0:T(8,128)(2,1)S(1)} %get-tuple-element.13), channel_id=1, source_target_pairs={{0,9},{1,8},{2,11},{3,10},{4,13},{5,12},{6,15},{7,14},{8,1},{9,0},... | collective-permute-start | bytes 393224 | tf_op jit(solution)/shard_map/ppermute | solution.py:27
  30.1 22.6 %collective-permute-start.9 = (bf16[1,1,32,2048]{3,2,1,0:T(8,128)(2,1)S(1)}, bf16[1,1,32,2048]{3,2,1,0:T(8,128)(2,1)S(1)}, u32[]{:S(2)}, u32[]{:S(2)}) collective-permute-start(bf16[1,1,32,2048]{3,2,1,0:T(8,128)(2,1)S(1)} %get-tuple-element.12), channel_id=1, source_target_pairs={{0,10},{1,11},{2,8},{3,9},{4,14},{5,15},{6,12},{7,13},{8,2},{9,3},... | collective-permute-start | bytes 393224 | tf_op jit(solution)/shard_map/ppermute | solution.py:27
  33.7 24.4 %collective-permute-start.10 = (bf16[1,1,32,2048]{3,2,1,0:T(8,128)(2,1)S(1)}, bf16[1,1,32,2048]{3,2,1,0:T(8,128)(2,1)S(1)}, u32[]{:S(2)}, u32[]{:S(2)}) collective-permute-start(bf16[1,1,32,2048]{3,2,1,0:T(8,128)(2,1)S(1)} %get-tuple-element.11), channel_id=1, source_target_pairs={{0,11},{1,10},{2,9},{3,8},{4,15},{5,14},{6,13},{7,12},{8,3},{9,2},... | collective-permute-start | bytes 393224 | tf_op jit(solution)/shard_map/ppermute | solution.py:27
  37.7 28.2 %collective-permute-start.11 = (bf16[1,1,32,2048]{3,2,1,0:T(8,128)(2,1)S(1)}, bf16[1,1,32,2048]{3,2,1,0:T(8,128)(2,1)S(1)}, u32[]{:S(2)}, u32[]{:S(2)}) collective-permute-start(bf16[1,1,32,2048]{3,2,1,0:T(8,128)(2,1)S(1)} %get-tuple-element.10), channel_id=1, source_target_pairs={{0,12},{1,13},{2,14},{3,15},{4,8},{5,9},{6,10},{7,11},{8,4},{9,5},... | collective-permute-start | bytes 393224 | tf_op jit(solution)/shard_map/ppermute | solution.py:27
  38.9 29.8 %collective-permute-start.12 = (bf16[1,1,32,2048]{3,2,1,0:T(8,128)(2,1)S(1)}, bf16[1,1,32,2048]{3,2,1,0:T(8,128)(2,1)S(1)}, u32[]{:S(2)}, u32[]{:S(2)}) collective-permute-start(bf16[1,1,32,2048]{3,2,1,0:T(8,128)(2,1)S(1)} %get-tuple-element.9), channel_id=1, source_target_pairs={{0,13},{1,12},{2,15},{3,14},{4,9},{5,8},{6,11},{7,10},{8,5},{9,4},... | collective-permute-start | bytes 393224 | tf_op jit(solution)/shard_map/ppermute | solution.py:27
  49.6 22.5 %collective-permute-start.13 = (bf16[1,1,32,2048]{3,2,1,0:T(8,128)(2,1)S(1)}, bf16[1,1,32,2048]{3,2,1,0:T(8,128)(2,1)S(1)}, u32[]{:S(2)}, u32[]{:S(2)}) collective-permute-start(bf16[1,1,32,2048]{3,2,1,0:T(8,128)(2,1)S(1)} %get-tuple-element.8), channel_id=1, source_target_pairs={{0,14},{1,15},{2,12},{3,13},{4,10},{5,11},{6,8},{7,9},{8,6},{9,7},... | collective-permute-start | bytes 393224 | tf_op jit(solution)/shard_map/ppermute | solution.py:27
  52.6 22.2 %collective-permute-start.14 = (bf16[1,1,32,2048]{3,2,1,0:T(8,128)(2,1)S(1)}, bf16[1,1,32,2048]{3,2,1,0:T(8,128)(2,1)S(1)}, u32[]{:S(2)}, u32[]{:S(2)}) collective-permute-start(bf16[1,1,32,2048]{3,2,1,0:T(8,128)(2,1)S(1)} %get-tuple-element.7), channel_id=1, source_target_pairs={{0,15},{1,14},{2,13},{3,12},{4,11},{5,10},{6,9},{7,8},{8,7},{9,6},... | collective-permute-start | bytes 393224 | tf_op jit(solution)/shard_map/ppermute | solution.py:27
  79.1 4.5 %copy-start.1 = (bf16[16,32,2048]{2,1,0:T(8,128)(2,1)S(1)}, bf16[16,32,2048]{2,1,0:T(8,128)(2,1)}, u32[]{:S(2)}) copy-start(bf16[16,32,2048]{2,1,0:T(8,128)(2,1)} %gather_fusion.1) | copy-start | bytes 6291460
  79.1 4.5 %copy-start.3 = (bf16[1,2048,768]{2,1,0:T(8,128)(2,1)S(1)}, bf16[1,2048,768]{2,1,0:T(8,128)(2,1)}, u32[]{:S(2)}) copy-start(bf16[1,2048,768]{2,1,0:T(8,128)(2,1)} %param.10) | copy-start | bytes 9437188
  88.6 4.7 %copy-start.2 = (f32[128,8]{0,1:T(8,128)S(1)}, f32[128,8]{0,1:T(8,128)}, u32[]{:S(2)}) copy-start(f32[128,8]{0,1:T(8,128)} %param.8) | copy-start | bytes 12292
  88.6 52.4 %all-to-all-start = ((bf16[1,16,32,2048]{3,2,0,1:T(8,128)(2,1)}), bf16[1,16,32,2048]{3,2,0,1:T(8,128)(2,1)}, u32[]{:S(2)}, u32[]{:S(2)}) async-start(bf16[1,16,32,2048]{3,2,0,1:T(8,128)(2,1)} %convolution_bitcast_fusion), calls=%async_computation | async-start | bytes 4194304 | tf_op jit(solution)/shard_map/all_to_all | solution.py:62
